TPU v7x, 256 devices: a whole 4x4x8 slice. The times are simulated.
256 devices in a mesh: win: 32 (over y, x, core), grp: 8 (over z).
Axes of the slice: x: 4, y: 4, z: 8, core: 2. Of those that a mesh axis runs over, the one named last changes fastest.
Arguments:
- traces: bfloat16 [256, 512, 2048], P(('win', 'grp'))
- pair_lists: int32 [32, 3], P('win'), may hold values from -1 to 3, as said below
- observed: float32 [32, 3, 16, 16, 2048], P('win'), may hold values from -4 to 4
Outputs:
- correl: float32 [32, 3, 16, 16, 2048], P('win', None, None, None, 'grp')
- trace_gradient: bfloat16 [256, 512, 2048], P(('win', 'grp'))
Inputs may be any that keep to these rules, and one draw needn't show every extreme that they name: `pair_lists`: each row lists distinct offsets in increasing order, followed by -1 in its empty slots; block a lists only offsets o with a + o < 32; every block lists at least one offset, and block 0 fills all 3 slots and lists offset 4 - 1.
All inputs are finite; a program needn't handle non-finite values.
Results may differ from a plain program's by a relative error of at most 0.014.
Values may be sent and summed in bfloat16 or wider, within the bound.
No kernel may reach another device: no remote copies, remote signals or barrier semaphores. Data moves between devices by JAX's collectives and lax.ppermute only.
A program may use at most 192 MiB of HBM per device.

v0:
```python
import math
import jax
import jax.numpy as jnp
from jax import lax
from jax.sharding import PartitionSpec as P

SEG = 2048
FREQ = 1024
BAND = 64
OFFSETS = 4


def passed_along(array, axis, by):
    peers = lax.axis_size(axis)
    pairs = [(i, i + by) for i in range(peers) if 0 <= i + by < peers]
    return lax.ppermute(array, axis, pairs)


def dft_table(first_column, column_count):
    samples = jnp.arange(SEG, dtype=jnp.int32)
    columns = first_column + jnp.arange(column_count, dtype=jnp.int32)
    harmonic = columns % FREQ
    phases = samples[:, None] * harmonic[None, :] % SEG
    angles = phases.astype(jnp.float32) * (2.0 * math.pi / SEG)
    values = jnp.where(columns[None, :] < FREQ, jnp.cos(angles), -jnp.sin(angles))
    return values.astype(jnp.bfloat16)


def whiten(spectrum):
    halfway = spectrum.shape[-1] // 2
    real_part = spectrum[..., :halfway]
    imag_part = spectrum[..., halfway:]
    power_bins = real_part * real_part + imag_part * imag_part
    banded = power_bins.reshape(power_bins.shape[:-1] + (halfway // BAND, BAND))
    inverse = lax.rsqrt(jnp.mean(banded, axis=-1) + 1e-05)
    spread = jnp.broadcast_to(inverse[..., None], banded.shape).reshape(power_bins.shape)
    return spectrum * jnp.concatenate([spread, spread], axis=-1)


def split_halves(operand):
    halfway = operand.shape[-1] // 2
    return (operand[..., :halfway], operand[..., halfway:])


def widen(operand):
    return operand.astype(jnp.float32)


def correlate(leading, trailing, windows_total):
    lead_real, lead_imag = split_halves(leading)
    trail_real, trail_imag = split_halves(trailing)
    left_real = widen(lead_real)[:, :, None, :]
    left_imag = widen(lead_imag)[:, :, None, :]
    right_real = widen(trail_real)[:, None, :, :]
    right_imag = widen(trail_imag)[:, None, :, :]
    real_sum = jnp.sum(left_real * right_real + left_imag * right_imag, axis=0)
    imag_sum = jnp.sum(left_real * right_imag - left_imag * right_real, axis=0)
    return jnp.concatenate([real_sum, imag_sum], axis=-1) / windows_total


def pull_first(residual, trailing):
    resid_real, resid_imag = split_halves(residual)
    trail_real, trail_imag = split_halves(trailing)
    left_real = widen(resid_real)[None]
    left_imag = widen(resid_imag)[None]
    right_real = widen(trail_real)[:, None, :, :]
    right_imag = widen(trail_imag)[:, None, :, :]
    real_part = jnp.sum(left_real * right_real + left_imag * right_imag, axis=2)
    imag_part = jnp.sum(left_real * right_imag - left_imag * right_real, axis=2)
    return jnp.concatenate([real_part, imag_part], axis=-1)


def pull_second(residual, leading):
    resid_real, resid_imag = split_halves(residual)
    lead_real, lead_imag = split_halves(leading)
    left_real = widen(resid_real)[None]
    left_imag = widen(resid_imag)[None]
    right_real = widen(lead_real)[:, :, None, :]
    right_imag = widen(lead_imag)[:, :, None, :]
    real_part = jnp.sum(left_real * right_real - left_imag * right_imag, axis=1)
    imag_part = jnp.sum(left_real * right_imag + left_imag * right_real, axis=1)
    return jnp.concatenate([real_part, imag_part], axis=-1)


def on_device(traces, pair_lists, observed):
    win_dev, channels, samples = traces.shape
    column_total = 2 * FREQ
    column_step = min(512, column_total)
    tables = [
        dft_table(start_col, column_step) for start_col in range(0, column_total, column_step)
    ]
    flat_traces = traces.reshape(win_dev * channels, samples)
    spectra = jnp.concatenate(
        [
            jnp.dot(flat_traces, table_part, preferred_element_type=jnp.float32)
            for table_part in tables
        ],
        axis=1,
    )
    spectra = spectra.reshape(win_dev, channels, column_total)
    whitened = whiten(spectra).astype(jnp.bfloat16)
    grp_count = lax.axis_size("grp")
    share_width = column_total // grp_count
    moved_blocks = lax.all_to_all(whitened, "win", split_axis=1, concat_axis=0, tiled=True)
    windows_total = moved_blocks.shape[0] * grp_count
    partner_list = [moved_blocks] + [
        passed_along(moved_blocks, "win", -offset) for offset in range(1, OFFSETS)
    ]
    stacked = jnp.stack(partner_list)
    offsets = pair_lists[0]
    slot_total = offsets.shape[0]
    live_slots = (offsets >= 0).astype(jnp.float32)[:, None, None, None]
    partners = [
        lax.dynamic_index_in_dim(stacked, jnp.maximum(offsets[slot_index], 0), 0, keepdims=False)
        for slot_index in range(slot_total)
    ]
    correl = (
        jnp.stack(
            [correlate(moved_blocks, partner_block, windows_total) for partner_block in partners]
        )
        * live_slots
    )
    share_start = lax.axis_index("grp") * share_width
    totals = lax.psum(correl, "grp")
    correl_share = lax.dynamic_slice_in_dim(totals, share_start, share_width, 3)
    residual = ((totals - observed[0]) * live_slots).astype(jnp.bfloat16)
    own_grad = pull_first(residual[0], partners[0])
    for slot_index in range(1, slot_total):
        own_grad = own_grad + pull_first(residual[slot_index], partners[slot_index])
    contrib = []
    for offset in range(OFFSETS):
        chosen = jnp.zeros_like(residual[0])
        for slot_index in range(slot_total):
            chosen = jnp.where(offsets[slot_index] == offset, residual[slot_index], chosen)
        contrib.append(pull_second(chosen, moved_blocks))
    white_grad = own_grad + contrib[0]
    for offset in range(1, OFFSETS):
        white_grad = white_grad + passed_along(
            contrib[offset].astype(jnp.bfloat16), "win", offset
        ).astype(jnp.float32)
    returned = lax.all_to_all(
        white_grad.astype(jnp.bfloat16), "win", split_axis=0, concat_axis=1, tiled=True
    )
    unused, pullback = jax.vjp(whiten, spectra)
    spectra_grad = pullback(returned.astype(jnp.float32))[0].astype(jnp.bfloat16)
    flat_grad = spectra_grad.reshape(win_dev * channels, column_total)
    trace_grad = jnp.zeros((win_dev * channels, samples), jnp.float32)
    for table_index in range(len(tables)):
        start_col = table_index * column_step
        trace_grad = trace_grad + jnp.dot(
            flat_grad[:, start_col : start_col + column_step],
            tables[table_index].T,
            preferred_element_type=jnp.float32,
        )
    return (correl_share[None], trace_grad.reshape(win_dev, channels, samples).astype(jnp.bfloat16))


def solution(mesh):
    return jax.shard_map(
        on_device,
        mesh=mesh,
        in_specs=(P(("win", "grp"), None, None), P("win", None), P("win", None, None, None, None)),
        out_specs=(P("win", None, None, None, "grp"), P(("win", "grp"), None, None)),
        check_vma=False,
    )
```

profile of v0, /device:TPU:1, one launch (start us, length us, event | category | flops | bytes accessed | tf_op | source)
XLA Modules:
  0.0 817.0 jit_solution(5095351248463171921)
XLA Ops:
  8.8 17.5 %fusion.41 = f32[512,512]{1,0:T(8,128)S(1)} fusion(bf16[1,512,2048]{2,1,0:T(8,128)(2,1)S(1)} %copy-done, s32[512]{0:T(512)S(1)} %add_select_fusion.4, pred[512]{0:T(512)(128)(4,1)S(1)} %fusion.60), kind=kOutput, calls=%fused_computation.95 | convolution fusion | flops 1091567616 | bytes 3148288 | tf_op jit(solution)/shard_map/dot_general | solution.py:95
  26.2 17.2 %fusion.43 = f32[512,512]{1,0:T(8,128)S(1)} fusion(bf16[1,512,2048]{2,1,0:T(8,128)(2,1)S(1)} %copy-done, s32[512]{0:T(512)S(1)} %add_select_fusion.5, pred[512]{0:T(512)(128)(4,1)S(1)} %fusion.61), kind=kOutput, calls=%fused_computation.97 | convolution fusion | flops 1091567616 | bytes 3148288 | tf_op jit(solution)/shard_map/dot_general | solution.py:95
  43.4 17.6 %fusion.45 = f32[512,512]{1,0:T(8,128)S(1)} fusion(bf16[1,512,2048]{2,1,0:T(8,128)(2,1)S(1)} %copy-done, s32[512]{0:T(512)S(1)} %add_select_fusion.6, pred[512]{0:T(512)(128)(4,1)S(1)} %fusion.62), kind=kOutput, calls=%fused_computation.99 | convolution fusion | flops 1091567616 | bytes 3148288 | tf_op jit(solution)/shard_map/dot_general | solution.py:95
  61.0 17.2 %fusion.47 = f32[512,512]{1,0:T(8,128)S(1)} fusion(bf16[1,512,2048]{2,1,0:T(8,128)(2,1)S(1)} %copy-done, s32[512]{0:T(512)S(1)} %add_select_fusion.7, pred[512]{0:T(512)(128)(4,1)S(1)} %iota_compare_fusion), kind=kOutput, calls=%fused_computation.101 | convolution fusion | flops 1091567616 | bytes 3148288 | tf_op jit(solution)/shard_map/dot_general | solution.py:95
  82.7 3.9 fusion.16
  86.6 10.8 %copy.14 = bf16[1,512,2048]{2,0,1:T(2,128)(2,1)} copy(bf16[1,512,2048]{1,2,0:T(8,128)(2,1)} %fusion.16) | data formatting | bytes 4194304 | tf_op jit(solution)/shard_map/convert_element_type | solution.py:101
  98.0 13.2 %reduce.2 = bf16[512,2048]{1,0:T(8,128)(2,1)S(1)} reduce(bf16[512,1,2048]{2,1,0:T(2,128)(2,1)} %bitcast.118, bf16[]{:T(256)} %broadcast.306), dimensions={1}, to_apply=%bitcast.108.reduce_sub_computation | reduce | bytes 4194306
  113.9 37.0 %all_to_all.21 = bf16[32,2,16384]{2,1,0:T(2,128)(2,1)S(1)} all-to-all(bf16[32,2,16384]{2,1,0:T(2,128)(2,1)} %reshape.499), channel_id=1, replica_groups=mesh['win'=32,'grp'=8] {'win'}, dimensions={0} | all-to-all | bytes 4194304 | tf_op jit(solution)/shard_map/all_to_all | solution.py:104
  150.9 6.8 reshape.500
  157.6 3.5 copy.17
  171.1 18.9 %collective-permute-done.2 = bf16[32,16,2048]{2,1,0:T(8,128)(2,1)S(1)} collective-permute-done((bf16[32,16,2048]{2,1,0:T(8,128)(2,1)S(1)}, bf16[32,16,2048]{2,1,0:T(8,128)(2,1)S(1)}, u32[]{:S(2)}, u32[]{:S(2)}) %collective-permute-start.2) | collective-permute-done | bytes 2097184 | tf_op jit(solution)/shard_map/ppermute | solution.py:16
  190.0 63.7 %collective-permute-done.1 = bf16[32,16,2048]{2,1,0:T(8,128)(2,1)S(1)} collective-permute-done((bf16[32,16,2048]{2,1,0:T(8,128)(2,1)S(1)}, bf16[32,16,2048]{2,1,0:T(8,128)(2,1)S(1)}, u32[]{:S(2)}, u32[]{:S(2)}) %collective-permute-start.1) | collective-permute-done | bytes 2097184 | tf_op jit(solution)/shard_map/ppermute | solution.py:16
  259.6 3.7 slice_convert_fusion
  263.3 35.8 %add_reduce_fusion.9 = (f32[16,16,1024]{2,1,0:T(8,128)}, f32[16,16,1024]{2,1,0:T(8,128)}, f32[16,16,1024]{2,1,0:T(8,128)}, f32[16,16,1024]{2,1,0:T(8,128)}, f32[16,16,1024]{2,1,0:T(8,128)}, /*index=5*/f32[16,16,1024]{2,1,0:T(8,128)}) fusion(f32[32,16,1024]{2,1,0:T(8,128)} %get-tuple-element.50, f32[32,16,1024]{2,1,0:T(8,128)} %get-tuple-element.48, ...), kind=kLoop, calls=%fused_computation.19 | loop fusion | flops 199753728 | bytes 23068672 | tf_op jit(solution)/shard_map/reduce_sum | solution.py:56
  313.0 164.2 %all-reduce.4.cloned.1.call-done = f32[3,16,16,2048]{3,2,1,0:T(8,128)} async-done(((f32[3,16,16,2048]{3,2,1,0:T(8,128)}), f32[3,16,16,2048]{3,2,1,0:T(8,128)}) %all-reduce.4.cloned.1.call-update) | async-done | bytes 6291472 | tf_op jit(solution)/shard_map/psum | solution.py:124
  477.2 6.4 fusion.1
  488.2 70.5 %subtract_reduce_fusion.2 = (bf16[32,16,1024]{2,1,0:T(8,128)(2,1)S(1)}, bf16[32,16,1024]{2,1,0:T(8,128)(2,1)S(1)}, f32[32,16,1024]{2,1,0:T(8,128)S(1)}, f32[32,1...) fusion(f32[16,16,1024]{2,1,0:T(8,128)S(1)} %get-tuple-element.5, ...), kind=kLoop, calls=%fused_computation.5 | loop fusion | flops 264241152 | bytes 23068672 | tf_op jit(solution)/shard_map/reduce_sum | solution.py:80
  560.6 6.5 collective-permute-start.5
  573.7 20.6 %add_reduce_fusion.4 = (f32[32,16,1024]{2,1,0:T(8,128)S(1)}, f32[32,16,1024]{2,1,0:T(8,128)S(1)}) fusion(f32[16,16,1024]{2,1,0:T(8,128)S(1)} %get-tuple-element.60, f32[16,16,1024]{2,1,0:T(8,128)S(1)} %get-tuple-element.59, f32[32,16,1024]{2,1,0:T(8,128)S(1)} %copy-done.9, f32[32,16,1024]{2,1,0:T(8,128)S(1)} %copy-done.10), kind=kLoop, calls=%fused_computation.9 | loop fusion | flops 66060288 | bytes 10485760 | tf_op jit(solution)/shard_map/reduce_sum | solution.py:68
  594.3 20.6 %add_reduce_fusion.5 = (f32[32,16,1024]{2,1,0:T(8,128)S(1)}, f32[32,16,1024]{2,1,0:T(8,128)S(1)}) fusion(f32[16,16,1024]{2,1,0:T(8,128)S(1)} %get-tuple-element.62, f32[16,16,1024]{2,1,0:T(8,128)S(1)} %get-tuple-element.61, f32[32,16,1024]{2,1,0:T(8,128)S(1)} %copy-done.8, f32[32,16,1024]{2,1,0:T(8,128)S(1)} %copy-done.7), kind=kLoop, calls=%fused_computation.11 | loop fusion | flops 66060288 | bytes 10485760 | tf_op jit(solution)/shard_map/reduce_sum | solution.py:68
  616.5 20.5 %add_reduce_fusion.6 = (f32[32,16,1024]{2,1,0:T(8,128)S(1)}, f32[32,16,1024]{2,1,0:T(8,128)S(1)}) fusion(f32[16,16,1024]{2,1,0:T(8,128)S(1)} %get-tuple-element.64, f32[16,16,1024]{2,1,0:T(8,128)S(1)} %get-tuple-element.63, f32[32,16,1024]{2,1,0:T(8,128)S(1)} %copy-done.4, f32[32,16,1024]{2,1,0:T(8,128)S(1)} %get-tuple-element.49), kind=kLoop, calls=%fused_computation.13 | loop fusion | flops 66060288 | bytes 10485760 | tf_op jit(solution)/shard_map/reduce_sum | solution.py:68
  637.1 17.6 %collective-permute-done.4 = bf16[32,16,2048]{2,1,0:T(8,128)(2,1)} collective-permute-done((bf16[32,16,2048]{2,1,0:T(8,128)(2,1)S(1)}, bf16[32,16,2048]{2,1,0:T(8,128)(2,1)}, u32[]{:S(2)}, u32[]{:S(2)}) %collective-permute-start.4) | collective-permute-done | bytes 2097184 | tf_op jit(solution)/shard_map/ppermute | solution.py:16
  654.6 22.6 %collective-permute-done.3 = bf16[32,16,2048]{2,1,0:T(8,128)(2,1)} collective-permute-done((bf16[32,16,2048]{2,1,0:T(8,128)(2,1)}, bf16[32,16,2048]{2,1,0:T(8,128)(2,1)}, u32[]{:S(2)}, u32[]{:S(2)}) %collective-permute-start.3) | collective-permute-done | bytes 2097184 | tf_op jit(solution)/shard_map/ppermute | solution.py:16
  677.2 5.7 fusion.25
  682.9 8.8 %all-to-all-start.1 = ((bf16[32,16,2048]{2,1,0:T(8,128)(2,1)}), bf16[32,16,2048]{2,1,0:T(8,128)(2,1)S(1)}, u32[]{:S(2)}, u32[]{:S(2)}) async-start(bf16[32,16,2048]{2,1,0:T(8,128)(2,1)} %fusion.25), calls=%async_computation.1 | async-start | bytes 4194304 | tf_op jit(solution)/shard_map/all_to_all | solution.py:141
  693.8 25.7 %all-to-all-done.1 = bf16[32,16,2048]{2,1,0:T(8,128)(2,1)S(1)} async-done(((bf16[32,16,2048]{2,1,0:T(8,128)(2,1)}), bf16[32,16,2048]{2,1,0:T(8,128)(2,1)S(1)}, u32[]{:S(2)}, u32[]{:S(2)}) %all-to-all-start.1) | async-done | bytes 2097184 | tf_op jit(solution)/shard_map/all_to_all | solution.py:141
  721.9 5.5 copy.15
  727.4 3.5 fusion.39
  737.3 17.7 %fusion.49 = f32[512,2048]{1,0:T(8,128)S(1)} fusion(s32[512]{0:T(512)S(1)} %add_select_fusion.5, pred[512]{0:T(512)(128)(4,1)S(1)} %fusion.61, bf16[512,2048]{0,1:T(8,128)(2,1)S(1)} %fusion.40), kind=kOutput, calls=%fused_computation.107 | convolution fusion | flops 1091567616 | bytes 4721152 | tf_op jit(solution)/shard_map/dot_general | solution.py:150
  755.0 17.8 %fusion.50 = f32[512,2048]{1,0:T(8,128)S(1)} fusion(s32[512]{0:T(512)S(1)} %add_select_fusion.6, pred[512]{0:T(512)(128)(4,1)S(1)} %fusion.62, bf16[512,2048]{0,1:T(8,128)(2,1)S(1)} %fusion.40), kind=kOutput, calls=%fused_computation.108 | convolution fusion | flops 1091567616 | bytes 4721152 | tf_op jit(solution)/shard_map/dot_general | solution.py:150
  772.8 18.1 %fusion.51 = f32[512,2048]{1,0:T(8,128)S(1)} fusion(s32[512]{0:T(512)S(1)} %add_select_fusion.7, pred[512]{0:T(512)(128)(4,1)S(1)} %iota_compare_fusion, bf16[512,2048]{0,1:T(8,128)(2,1)S(1)} %fusion.40), kind=kOutput, calls=%fused_computation.109 | convolution fusion | flops 1091567616 | bytes 4721152 | tf_op jit(solution)/shard_map/dot_general | solution.py:150
  791.0 19.0 %fusion.38 = bf16[1,512,2048]{2,1,0:T(8,128)(2,1)} fusion(f32[512,2048]{1,0:T(8,128)S(1)} %fusion.49, f32[512,2048]{1,0:T(8,128)S(1)} %fusion.51, f32[512,2048]{1,0:T(8,128)S(1)} %fusion.50, s32[512]{0:T(512)S(1)} %add_select_fusion.4, pred[512]{0:T(512)(128)(4,1)S(1)} %fusion.60, bf16[512,2048]{0,1:T(8,128)(2,1)S(1)} %fusion.40), kind=kOutput, calls=%fused_computation.84 | convolution fusion | flops 1095761920 | bytes 15206912 | tf_op jit(solution)/shard_map/dot_general | solution.py:150
  (106 shorter events, 55.0 us)
Async XLA Ops:
  7.2 1.6 copy-start
  7.2 470.0 %all-reduce.4.cloned.1.call-start = ((), (), s32[]{:S(2)}) async-start(), calls=%async_computation.2 | async-start | bytes 12582912 | tf_op jit(solution)/shard_map/psum | solution.py:124
  43.4 34.8 %copy-start.13 = (f32[512,512]{1,0:T(8,128)}, f32[512,512]{1,0:T(8,128)S(1)}, u32[]{:S(2)}) copy-start(f32[512,512]{1,0:T(8,128)S(1)} %fusion.43) | copy-start | bytes 3145732
  61.0 17.2 %copy-start.15 = (f32[512,512]{1,0:T(8,128)}, f32[512,512]{1,0:T(8,128)S(1)}, u32[]{:S(2)}) copy-start(f32[512,512]{1,0:T(8,128)S(1)} %fusion.45) | copy-start | bytes 3145732
  79.2 2.0 copy-start.3
  82.6 3.9 copy-start.5
  157.6 8.4 %copy-start.25 = (s32[1,3]{1,0:T(1,128)S(1)}, s32[1,3]{1,0:T(1,128)}, u32[]{:S(2)}) copy-start(s32[1,3]{1,0:T(1,128)} %param.4) | copy-start | bytes 40
  161.1 28.9 %collective-permute-start.2 = (bf16[32,16,2048]{2,1,0:T(8,128)(2,1)S(1)}, bf16[32,16,2048]{2,1,0:T(8,128)(2,1)S(1)}, u32[]{:S(2)}, u32[]{:S(2)}) collective-permute-start(bf16[32,16,2048]{2,1,0:T(8,128)(2,1)S(1)} %bitcast.111), channel_id=1, source_target_pairs={{24,0},{32,8},{40,16},{48,24},{56,32},{64,40},{72,48},{80,56},{88,... | collective-permute-start | bytes 6291464 | tf_op jit(solution)/shard_map/ppermute | solution.py:16
  162.4 91.2 %collective-permute-start.1 = (bf16[32,16,2048]{2,1,0:T(8,128)(2,1)S(1)}, bf16[32,16,2048]{2,1,0:T(8,128)(2,1)S(1)}, u32[]{:S(2)}, u32[]{:S(2)}) collective-permute-start(bf16[32,16,2048]{2,1,0:T(8,128)(2,1)S(1)} %bitcast.112), channel_id=1, source_target_pairs={{16,0},{24,8},{32,16},{40,24},{48,32},{56,40},{64,48},{72,56},{80,... | collective-permute-start | bytes 6291464 | tf_op jit(solution)/shard_map/ppermute | solution.py:16
  163.7 91.9 %collective-permute-start = (bf16[32,16,2048]{2,1,0:T(8,128)(2,1)S(1)}, bf16[32,16,2048]{2,1,0:T(8,128)(2,1)S(1)}, u32[]{:S(2)}, u32[]{:S(2)}) collective-permute-start(bf16[32,16,2048]{2,1,0:T(8,128)(2,1)S(1)} %bitcast.113), channel_id=1, source_target_pairs={{8,0},{16,8},{24,16},{32,24},{40,32},{48,40},{56,48},{64,56},{72,6... | collective-permute-start | bytes 6291464 | tf_op jit(solution)/shard_map/ppermute | solution.py:16
  299.1 1.9 copy-start.23
  299.1 2.2 copy-start.24
  299.1 2.5 copy-start.21
  299.1 2.8 copy-start.22
  486.0 2.2 copy-start.12
  558.7 8.4 %copy-start.19 = (bf16[32,16,1024]{2,1,0:T(8,128)(2,1)S(1)}, bf16[32,16,1024]{2,1,0:T(8,128)(2,1)}, u32[]{:S(2)}) copy-start(bf16[32,16,1024]{2,1,0:T(8,128)(2,1)} %get-tuple-element.24) | copy-start | bytes 3145732
  558.7 8.4 %copy-start.20 = (bf16[32,16,1024]{2,1,0:T(8,128)(2,1)S(1)}, bf16[32,16,1024]{2,1,0:T(8,128)(2,1)}, u32[]{:S(2)}) copy-start(bf16[32,16,1024]{2,1,0:T(8,128)(2,1)} %get-tuple-element.25) | copy-start | bytes 3145732
  560.6 76.5 %collective-permute-start.5 = (bf16[32,16,2048]{2,1,0:T(8,128)(2,1)S(1)}, bf16[32,16,2048]{2,1,0:T(8,128)(2,1)}, u32[]{:S(2)}, u32[]{:S(2)}) collective-permute-start(bf16[32,16,2048]{2,1,0:T(8,128)(2,1)S(1)} %pad_maximum_fusion.5), channel_id=1, source_target_pairs={{0,24},{8,32},{16,40},{24,48},{32,56},{40,64},{48,72},{56,80},{64,... | collective-permute-start | bytes 6291464 | tf_op jit(solution)/shard_map/ppermute | solution.py:16
  567.1 6.6 copy-start.9
  567.1 6.6 copy-start.10
  567.3 87.3 %collective-permute-start.4 = (bf16[32,16,2048]{2,1,0:T(8,128)(2,1)S(1)}, bf16[32,16,2048]{2,1,0:T(8,128)(2,1)}, u32[]{:S(2)}, u32[]{:S(2)}) collective-permute-start(bf16[32,16,2048]{2,1,0:T(8,128)(2,1)S(1)} %pad_maximum_fusion.4), channel_id=1, source_target_pairs={{0,16},{8,24},{16,32},{24,40},{32,48},{40,56},{48,64},{56,72},{64,... | collective-permute-start | bytes 6291464 | tf_op jit(solution)/shard_map/ppermute | solution.py:16
  571.7 105.5 %collective-permute-start.3 = (bf16[32,16,2048]{2,1,0:T(8,128)(2,1)}, bf16[32,16,2048]{2,1,0:T(8,128)(2,1)}, u32[]{:S(2)}, u32[]{:S(2)}) collective-permute-start(bf16[32,16,2048]{2,1,0:T(8,128)(2,1)} %pad_maximum_fusion.3), channel_id=1, source_target_pairs={{0,8},{8,16},{16,24},{24,32},{32,40},{40,48},{48,56},{56,64},{64,7... | collective-permute-start | bytes 6291464 | tf_op jit(solution)/shard_map/ppermute | solution.py:16
  573.7 20.6 %copy-start.7 = (f32[32,16,1024]{2,1,0:T(8,128)S(1)}, f32[32,16,1024]{2,1,0:T(8,128)}, u32[]{:S(2)}) copy-start(f32[32,16,1024]{2,1,0:T(8,128)} %get-tuple-element.68) | copy-start | bytes 6291460
  573.7 20.6 %copy-start.8 = (f32[32,16,1024]{2,1,0:T(8,128)S(1)}, f32[32,16,1024]{2,1,0:T(8,128)}, u32[]{:S(2)}) copy-start(f32[32,16,1024]{2,1,0:T(8,128)} %get-tuple-element.69) | copy-start | bytes 6291460
  594.3 20.6 %copy-start.18 = (bf16[16,16,2048]{2,1,0:T(8,128)(2,1)S(1)}, bf16[16,16,2048]{2,1,0:T(8,128)(2,1)}, u32[]{:S(2)}) copy-start(bf16[16,16,2048]{2,1,0:T(8,128)(2,1)} %get-tuple-element.42) | copy-start | bytes 3145732
  614.9 1.6 copy-start.4
  682.9 36.5 %all-to-all-start.1 = ((bf16[32,16,2048]{2,1,0:T(8,128)(2,1)}), bf16[32,16,2048]{2,1,0:T(8,128)(2,1)S(1)}, u32[]{:S(2)}, u32[]{:S(2)}) async-start(bf16[32,16,2048]{2,1,0:T(8,128)(2,1)} %fusion.25), calls=%async_computation.1 | async-start | bytes 4194304 | tf_op jit(solution)/shard_map/all_to_all | solution.py:141
  721.9 5.5 copy-start.14
  721.9 5.5 copy-start.16
  731.7 3.5 copy-start.2
  731.8 4.1 copy-start.6
  790.9 19.0 %copy-start.1 = (bf16[1,512,2048]{2,1,0:T(8,128)(2,1)S(1)}, bf16[1,512,2048]{2,1,0:T(8,128)(2,1)}, u32[]{:S(2)}) copy-start(bf16[1,512,2048]{2,1,0:T(8,128)(2,1)} %param.3) | copy-start | bytes 6291460
  (2 other events, 2.6 us)
Sparse Core Ops, SparseCore 0:
  305.7 171.4 all-reduce.3
where the time goes:
time: 826 us; the launch traced here: 817 us
  waiting for transfers between devices  315 us (38%)
  other arithmetic  230 us (28%)
  matrix products  142 us (17%)
  local copies, waits for them, and re-layouts  43.9 us (5%)
  blocking collectives  37 us (4%)
  starting transfers between devices  25.1 us (3%)
  between operations  24.1 us (3%)
    psum x1, waiting for transfers between devices, on_device(): totals = lax.psum(correl, 'grp')  164 us
    ppermute x6, waiting for transfers between devices, passed_along(): return lax.ppermute(array, axis, pairs)  125 us
    dot_general x4, matrix products, on_device(): jnp.dot(flat_grad[:, start_col:start_col + column_step], tables[table_ind...  72.6 us
    reduce_sum x1, other arithmetic, pull_second(): real_part = jnp.sum(left_real * right_real - left_imag * right_imag, axis=1)  70.5 us
    dot_general x4, matrix products, on_device(): jnp.dot(flat_traces, table_part, preferred_element_type=jnp.float32)  69.4 us
    reduce_sum x3, other arithmetic, pull_first(): real_part = jnp.sum(left_real * right_real + left_imag * right_imag, axis=2)  61.7 us
    all_to_all x1, blocking collectives, on_device(): lax.all_to_all(whitened, 'win', split_axis=1, concat_axis=0, tiled=True)  37 us
    reduce_sum x1, other arithmetic, correlate(): real_sum = jnp.sum(left_real * right_real + left_imag * right_imag, axis=0)  35.8 us
  transfers between devices with their start and end apart: 8, of which 7 were waited for; matrix products, arithmetic and copies ran while one was open for 8% of the time, Pallas kernels for 0%

commit v1 on v0

--- a/solution.py
+++ b/solution.py
@@ -121,7 +121,11 @@
         * live_slots
     )
     share_start = lax.axis_index("grp") * share_width
-    totals = lax.psum(correl, "grp")
+
+    def divide_core(v0):
+        return jnp.sum(lax.all_gather(v0, axis_name="grp"), axis=0)
+
+    totals = divide_core(correl)
     correl_share = lax.dynamic_slice_in_dim(totals, share_start, share_width, 3)
     residual = ((totals - observed[0]) * live_slots).astype(jnp.bfloat16)
     own_grad = pull_first(residual[0], partners[0])

time: 826 us -> 1190 us (1.44)
  waiting for transfers between devices: 315 us -> 654 us
  other arithmetic: 230 us -> 248 us
    all_gather x0 -> x1, waiting for transfers between devices: none -> 546 us  [divide_core(): return jnp.sum(lax.all_gather(v0, axis_name='grp'), axis=0)]
    psum x1 -> x0, waiting for transfers between devices: 164 us -> none  [on_device(): totals = lax.psum(correl, 'grp')]
    ppermute x6, waiting for transfers between devices: 125 us -> 82.2 us  [passed_along(): return lax.ppermute(array, axis, pairs)]
    reduce_sum x0 -> x1, other arithmetic: none -> 20.4 us  [divide_core(): return jnp.sum(lax.all_gather(v0, axis_name='grp'), axis=0)]
  transfers between devices with their start and end apart: 8 -> 8, of which waited for: 7 -> 6; matrix products, arithmetic and copies ran while one was open for 8% -> 6% of each run, Pallas kernels for 0% -> 0%
where the time goes in v1:
time: 1190 us; the launch traced here: 1180 us
  waiting for transfers between devices  654 us (55%)
  other arithmetic  248 us (21%)
  matrix products  142 us (12%)
  local copies, waits for them, and re-layouts  44.7 us (4%)
  blocking collectives  37 us (3%)
  starting transfers between devices  25.7 us (2%)
  between operations  24.7 us (2%)
    all_gather x1, waiting for transfers between devices, divide_core(): return jnp.sum(lax.all_gather(v0, axis_name='grp'), axis=0)  546 us
    ppermute x6, waiting for transfers between devices, passed_along(): return lax.ppermute(array, axis, pairs)  82.2 us
    dot_general x4, matrix products, on_device(): jnp.dot(flat_grad[:, start_col:start_col + column_step], tables[table_ind...  72.6 us
    reduce_sum x1, other arithmetic, pull_second(): real_part = jnp.sum(left_real * right_real - left_imag * right_imag, axis=1)  69.6 us
    dot_general x4, matrix products, on_device(): jnp.dot(flat_traces, table_part, preferred_element_type=jnp.float32)  69.4 us
    reduce_sum x3, other arithmetic, pull_first(): real_part = jnp.sum(left_real * right_real + left_imag * right_imag, axis=2)  61.7 us
    all_to_all x1, blocking collectives, on_device(): lax.all_to_all(whitened, 'win', split_axis=1, concat_axis=0, tiled=True)  37 us
    reduce_sum x1, other arithmetic, correlate(): real_sum = jnp.sum(left_real * right_real + left_imag * right_imag, axis=0)  35.8 us
  transfers between devices with their start and end apart: 8, of which 6 were waited for; matrix products, arithmetic and copies ran while one was open for 6% of the time, Pallas kernels for 0%

profile of v1, /device:TPU:1, one launch (start us, length us, event | category | flops | bytes accessed | tf_op | source)
XLA Modules:
  0.0 1176.3 jit_solution(3680514620451780739)
XLA Ops:
  8.8 17.5 %fusion.50 = f32[512,512]{1,0:T(8,128)S(1)} fusion(bf16[1,512,2048]{2,1,0:T(8,128)(2,1)S(1)} %copy-done, s32[512]{0:T(512)S(1)} %add_select_fusion.7, pred[512]{0:T(512)(128)(4,1)S(1)} %iota_compare_fusion), kind=kOutput, calls=%fused_computation.104 | convolution fusion | flops 1091567616 | bytes 3148288 | tf_op jit(solution)/shard_map/dot_general | solution.py:95
  26.2 17.2 %fusion.48 = f32[512,512]{1,0:T(8,128)S(1)} fusion(bf16[1,512,2048]{2,1,0:T(8,128)(2,1)S(1)} %copy-done, s32[512]{0:T(512)S(1)} %add_select_fusion.6, pred[512]{0:T(512)(128)(4,1)S(1)} %fusion.65), kind=kOutput, calls=%fused_computation.102 | convolution fusion | flops 1091567616 | bytes 3148288 | tf_op jit(solution)/shard_map/dot_general | solution.py:95
  43.4 17.6 %fusion.46 = f32[512,512]{1,0:T(8,128)S(1)} fusion(bf16[1,512,2048]{2,1,0:T(8,128)(2,1)S(1)} %copy-done, s32[512]{0:T(512)S(1)} %add_select_fusion.5, pred[512]{0:T(512)(128)(4,1)S(1)} %fusion.64), kind=kOutput, calls=%fused_computation.100 | convolution fusion | flops 1091567616 | bytes 3148288 | tf_op jit(solution)/shard_map/dot_general | solution.py:95
  61.0 17.2 %fusion.44 = f32[512,512]{1,0:T(8,128)S(1)} fusion(bf16[1,512,2048]{2,1,0:T(8,128)(2,1)S(1)} %copy-done, s32[512]{0:T(512)S(1)} %add_select_fusion.4, pred[512]{0:T(512)(128)(4,1)S(1)} %fusion.63), kind=kOutput, calls=%fused_computation.98 | convolution fusion | flops 1091567616 | bytes 3148288 | tf_op jit(solution)/shard_map/dot_general | solution.py:95
  82.8 4.0 fusion.16
  86.7 10.8 copy.14
  98.1 13.2 %reduce.2 = bf16[512,2048]{1,0:T(8,128)(2,1)S(1)} reduce(bf16[512,1,2048]{2,1,0:T(2,128)(2,1)} %bitcast.124, bf16[]{:T(256)} %broadcast.331), dimensions={1}, to_apply=%bitcast.114.reduce_sub_computation | reduce | bytes 4194306
  114.0 37.0 %all_to_all.21 = bf16[32,2,16384]{2,1,0:T(2,128)(2,1)S(1)} all-to-all(bf16[32,2,16384]{2,1,0:T(2,128)(2,1)} %reshape.595), channel_id=1, replica_groups=mesh['win'=32,'grp'=8] {'win'}, dimensions={0} | all-to-all | bytes 4194304 | tf_op jit(solution)/shard_map/all_to_all | solution.py:104
  151.0 6.8 reshape.596
  171.2 38.1 %collective-permute-done = bf16[32,16,2048]{2,1,0:T(8,128)(2,1)S(1)} collective-permute-done((bf16[32,16,2048]{2,1,0:T(8,128)(2,1)S(1)}, bf16[32,16,2048]{2,1,0:T(8,128)(2,1)S(1)}, u32[]{:S(2)}, u32[]{:S(2)}) %collective-permute-start) | collective-permute-done | bytes 2097184 | tf_op jit(solution)/shard_map/ppermute | solution.py:16
  209.3 3.9 collective-permute-done.1
  217.2 3.7 slice_convert_fusion
  220.9 35.8 %add_reduce_fusion.9 = (f32[16,16,1024]{2,1,0:T(8,128)}, f32[16,16,1024]{2,1,0:T(8,128)}, f32[16,16,1024]{2,1,0:T(8,128)}, f32[16,16,1024]{2,1,0:T(8,128)}, f32[16,16,1024]{2,1,0:T(8,128)}, /*index=5*/f32[16,16,1024]{2,1,0:T(8,128)}) fusion(f32[32,16,1024]{2,1,0:T(8,128)} %get-tuple-element.50, f32[32,16,1024]{2,1,0:T(8,128)} %get-tuple-element.48, ...), kind=kLoop, calls=%fused_computation.19 | loop fusion | flops 199753728 | bytes 23068672 | tf_op jit(solution)/shard_map/reduce_sum | solution.py:56
  270.9 546.0 %all-gather.2.cloned.1.call-done = f32[8,3,16,16,2048]{4,3,2,1,0:T(8,128)} async-done(((f32[1,3,16,16,2048]{4,3,2,1,0:T(8,128)}), f32[8,3,16,16,2048]{4,3,2,1,0:T(8,128)}) %all-gather.2.cloned.1.call-update) | async-done | bytes 50331664 | tf_op jit(solution)/shard_map/all_gather | solution.py:126
  816.9 20.4 %reduce_sum.222 = f32[3,16,16,2048]{3,2,1,0:T(8,128)} reduce(f32[8,3,16,16,2048]{4,3,2,1,0:T(8,128)} %all-gather.2.cloned.1.call-done, f32[]{:T(128)} %constant.114.clone.1), dimensions={0}, to_apply=%region_7.8 | reduce | flops 11010048 | bytes 56623108 | tf_op jit(solution)/shard_map/reduce_sum | solution.py:126
  837.3 6.4 fusion.1
  848.5 69.6 %subtract_reduce_fusion.2 = (bf16[32,16,1024]{2,1,0:T(8,128)(2,1)}, bf16[32,16,1024]{2,1,0:T(8,128)(2,1)}, f32[32,16,1024]{2,1,0:T(8,128)S(1)}, f32[32,16,1024]{...) fusion(f32[16,16,1024]{2,1,0:T(8,128)S(1)} %get-tuple-element.5, ...), kind=kLoop, calls=%fused_computation.5 | loop fusion | flops 264241152 | bytes 23068672 | tf_op jit(solution)/shard_map/reduce_sum | solution.py:80
  923.7 4.5 collective-permute-start.4
  928.5 3.7 collective-permute-start.5
  932.7 20.6 %add_reduce_fusion.4 = (f32[32,16,1024]{2,1,0:T(8,128)S(1)}, f32[32,16,1024]{2,1,0:T(8,128)S(1)}) fusion(f32[16,16,1024]{2,1,0:T(8,128)S(1)} %get-tuple-element.60, f32[16,16,1024]{2,1,0:T(8,128)S(1)} %get-tuple-element.59, f32[32,16,1024]{2,1,0:T(8,128)S(1)} %copy-done.9, f32[32,16,1024]{2,1,0:T(8,128)S(1)} %copy-done.10), kind=kLoop, calls=%fused_computation.9 | loop fusion | flops 66060288 | bytes 10485760 | tf_op jit(solution)/shard_map/reduce_sum | solution.py:68
  953.4 20.6 %add_reduce_fusion.5 = (f32[32,16,1024]{2,1,0:T(8,128)S(1)}, f32[32,16,1024]{2,1,0:T(8,128)S(1)}) fusion(f32[16,16,1024]{2,1,0:T(8,128)S(1)} %get-tuple-element.62, f32[16,16,1024]{2,1,0:T(8,128)S(1)} %get-tuple-element.61, f32[32,16,1024]{2,1,0:T(8,128)S(1)} %copy-done.8, f32[32,16,1024]{2,1,0:T(8,128)S(1)} %copy-done.7), kind=kLoop, calls=%fused_computation.11 | loop fusion | flops 66060288 | bytes 10485760 | tf_op jit(solution)/shard_map/reduce_sum | solution.py:68
  975.6 20.5 %add_reduce_fusion.6 = (f32[32,16,1024]{2,1,0:T(8,128)S(1)}, f32[32,16,1024]{2,1,0:T(8,128)S(1)}) fusion(f32[16,16,1024]{2,1,0:T(8,128)S(1)} %get-tuple-element.64, f32[16,16,1024]{2,1,0:T(8,128)S(1)} %get-tuple-element.63, f32[32,16,1024]{2,1,0:T(8,128)S(1)} %copy-done.4, f32[32,16,1024]{2,1,0:T(8,128)S(1)} %get-tuple-element.49), kind=kLoop, calls=%fused_computation.13 | loop fusion | flops 66060288 | bytes 10485760 | tf_op jit(solution)/shard_map/reduce_sum | solution.py:68
  996.1 14.9 %collective-permute-done.4 = bf16[32,16,2048]{2,1,0:T(8,128)(2,1)} collective-permute-done((bf16[32,16,2048]{2,1,0:T(8,128)(2,1)S(1)}, bf16[32,16,2048]{2,1,0:T(8,128)(2,1)}, u32[]{:S(2)}, u32[]{:S(2)}) %collective-permute-start.4) | collective-permute-done | bytes 2097184 | tf_op jit(solution)/shard_map/ppermute | solution.py:16
  1011.0 25.4 %collective-permute-done.5 = bf16[32,16,2048]{2,1,0:T(8,128)(2,1)} collective-permute-done((bf16[32,16,2048]{2,1,0:T(8,128)(2,1)S(1)}, bf16[32,16,2048]{2,1,0:T(8,128)(2,1)}, u32[]{:S(2)}, u32[]{:S(2)}) %collective-permute-start.5) | collective-permute-done | bytes 2097184 | tf_op jit(solution)/shard_map/ppermute | solution.py:16
  1036.4 5.7 fusion.25
  1042.1 8.9 all-to-all-start.1
  1053.0 25.7 %all-to-all-done.1 = bf16[32,16,2048]{2,1,0:T(8,128)(2,1)S(1)} async-done(((bf16[32,16,2048]{2,1,0:T(8,128)(2,1)}), bf16[32,16,2048]{2,1,0:T(8,128)(2,1)S(1)}, u32[]{:S(2)}, u32[]{:S(2)}) %all-to-all-start.1) | async-done | bytes 2097184 | tf_op jit(solution)/shard_map/all_to_all | solution.py:145
  1081.2 5.5 copy.15
  1096.6 17.7 %fusion.53 = f32[512,2048]{1,0:T(8,128)S(1)} fusion(s32[512]{0:T(512)S(1)} %add_select_fusion.6, pred[512]{0:T(512)(128)(4,1)S(1)} %fusion.65, bf16[512,2048]{0,1:T(8,128)(2,1)S(1)} %fusion.40), kind=kOutput, calls=%fused_computation.111 | convolution fusion | flops 1091567616 | bytes 4721152 | tf_op jit(solution)/shard_map/dot_general | solution.py:154
  1114.3 17.8 %fusion.54 = f32[512,2048]{1,0:T(8,128)S(1)} fusion(s32[512]{0:T(512)S(1)} %copy-done.26, pred[512]{0:T(512)(128)(4,1)S(1)} %copy-done.28, bf16[512,2048]{0,1:T(8,128)(2,1)S(1)} %fusion.40), kind=kOutput, calls=%fused_computation.112 | convolution fusion | flops 1091567616 | bytes 4721152 | tf_op jit(solution)/shard_map/dot_general | solution.py:154
  1132.1 18.1 %fusion.52 = f32[512,2048]{1,0:T(8,128)S(1)} fusion(s32[512]{0:T(512)S(1)} %add_select_fusion.5, pred[512]{0:T(512)(128)(4,1)S(1)} %fusion.64, bf16[512,2048]{0,1:T(8,128)(2,1)S(1)} %fusion.40), kind=kOutput, calls=%fused_computation.110 | convolution fusion | flops 1091567616 | bytes 4721152 | tf_op jit(solution)/shard_map/dot_general | solution.py:154
  1150.3 19.0 %fusion.38 = bf16[1,512,2048]{2,1,0:T(8,128)(2,1)} fusion(f32[512,2048]{1,0:T(8,128)S(1)} %fusion.52, f32[512,2048]{1,0:T(8,128)S(1)} %fusion.54, f32[512,2048]{1,0:T(8,128)S(1)} %fusion.53, s32[512]{0:T(512)S(1)} %add_select_fusion.4, pred[512]{0:T(512)(128)(4,1)S(1)} %fusion.63, bf16[512,2048]{0,1:T(8,128)(2,1)S(1)} %fusion.40), kind=kOutput, calls=%fused_computation.84 | convolution fusion | flops 1095761920 | bytes 15206912 | tf_op jit(solution)/shard_map/dot_general | solution.py:154
  (113 shorter events, 57.9 us)
Async XLA Ops:
  7.2 809.8 %all-gather.2.cloned.1.call-start = ((), (), s32[]{:S(2)}) async-start(), calls=%async_computation.2 | async-start | bytes 56623104 | tf_op jit(solution)/shard_map/all_gather | solution.py:126
  7.2 19.0 %copy-start.25 = (s32[512]{0:T(512)}, s32[512]{0:T(512)S(1)}, u32[]{:S(2)}) copy-start(s32[512]{0:T(512)S(1)} %add_select_fusion.7) | copy-start | bytes 6148
  7.3 19.0 %copy-start.27 = (pred[512]{0:T(512)(128)(4,1)}, pred[512]{0:T(512)(128)(4,1)S(1)}, u32[]{:S(2)}) copy-start(pred[512]{0:T(512)(128)(4,1)S(1)} %iota_compare_fusion) | copy-start | bytes 1540
  43.4 34.8 %copy-start.13 = (f32[512,512]{1,0:T(8,128)}, f32[512,512]{1,0:T(8,128)S(1)}, u32[]{:S(2)}) copy-start(f32[512,512]{1,0:T(8,128)S(1)} %fusion.48) | copy-start | bytes 3145732
  61.0 17.2 %copy-start.15 = (f32[512,512]{1,0:T(8,128)}, f32[512,512]{1,0:T(8,128)S(1)}, u32[]{:S(2)}) copy-start(f32[512,512]{1,0:T(8,128)S(1)} %fusion.46) | copy-start | bytes 3145732
  79.3 2.0 copy-start.3
  82.7 4.0 copy-start.5
  157.8 8.4 copy-start.24
  161.2 48.0 %collective-permute-start = (bf16[32,16,2048]{2,1,0:T(8,128)(2,1)S(1)}, bf16[32,16,2048]{2,1,0:T(8,128)(2,1)S(1)}, u32[]{:S(2)}, u32[]{:S(2)}) collective-permute-start(bf16[32,16,2048]{2,1,0:T(8,128)(2,1)S(1)} %bitcast.117), channel_id=1, source_target_pairs={{8,0},{16,8},{24,16},{32,24},{40,32},{48,40},{56,48},{64,56},{72,6... | collective-permute-start | bytes 6291464 | tf_op jit(solution)/shard_map/ppermute | solution.py:16
  163.6 49.6 %collective-permute-start.1 = (bf16[32,16,2048]{2,1,0:T(8,128)(2,1)S(1)}, bf16[32,16,2048]{2,1,0:T(8,128)(2,1)S(1)}, u32[]{:S(2)}, u32[]{:S(2)}) collective-permute-start(bf16[32,16,2048]{2,1,0:T(8,128)(2,1)S(1)} %bitcast.118), channel_id=1, source_target_pairs={{16,0},{24,8},{32,16},{40,24},{48,32},{56,40},{64,48},{72,56},{80,... | collective-permute-start | bytes 6291464 | tf_op jit(solution)/shard_map/ppermute | solution.py:16
  164.9 48.3 %collective-permute-start.2 = (bf16[32,16,2048]{2,1,0:T(8,128)(2,1)S(1)}, bf16[32,16,2048]{2,1,0:T(8,128)(2,1)S(1)}, u32[]{:S(2)}, u32[]{:S(2)}) collective-permute-start(bf16[32,16,2048]{2,1,0:T(8,128)(2,1)S(1)} %bitcast.119), channel_id=1, source_target_pairs={{24,0},{32,8},{40,16},{48,24},{56,32},{64,40},{72,48},{80,56},{88,... | collective-permute-start | bytes 6291464 | tf_op jit(solution)/shard_map/ppermute | solution.py:16
  256.7 2.2 copy-start.23
  256.7 2.5 copy-start.20
  256.7 2.8 copy-start.21
  846.3 2.2 copy-start.12
  919.9 76.3 %collective-permute-start.3 = (bf16[32,16,2048]{2,1,0:T(8,128)(2,1)S(1)}, bf16[32,16,2048]{2,1,0:T(8,128)(2,1)}, u32[]{:S(2)}, u32[]{:S(2)}) collective-permute-start(bf16[32,16,2048]{2,1,0:T(8,128)(2,1)S(1)} %pad_maximum_fusion.3), channel_id=1, source_target_pairs={{0,8},{8,16},{16,24},{24,32},{32,40},{40,48},{48,56},{56,64},{64,7... | collective-permute-start | bytes 6291464 | tf_op jit(solution)/shard_map/ppermute | solution.py:16
  923.7 8.7 copy-start.19
  923.7 87.3 %collective-permute-start.4 = (bf16[32,16,2048]{2,1,0:T(8,128)(2,1)S(1)}, bf16[32,16,2048]{2,1,0:T(8,128)(2,1)}, u32[]{:S(2)}, u32[]{:S(2)}) collective-permute-start(bf16[32,16,2048]{2,1,0:T(8,128)(2,1)S(1)} %pad_maximum_fusion.4), channel_id=1, source_target_pairs={{0,16},{8,24},{16,32},{24,40},{32,48},{40,56},{48,64},{56,72},{64,... | collective-permute-start | bytes 6291464 | tf_op jit(solution)/shard_map/ppermute | solution.py:16
  928.4 4.3 copy-start.9
  928.5 4.3 copy-start.10
  928.5 107.9 %collective-permute-start.5 = (bf16[32,16,2048]{2,1,0:T(8,128)(2,1)S(1)}, bf16[32,16,2048]{2,1,0:T(8,128)(2,1)}, u32[]{:S(2)}, u32[]{:S(2)}) collective-permute-start(bf16[32,16,2048]{2,1,0:T(8,128)(2,1)S(1)} %pad_maximum_fusion.5), channel_id=1, source_target_pairs={{0,24},{8,32},{16,40},{24,48},{32,56},{40,64},{48,72},{56,80},{64,... | collective-permute-start | bytes 6291464 | tf_op jit(solution)/shard_map/ppermute | solution.py:16
  932.7 20.6 %copy-start.7 = (f32[32,16,1024]{2,1,0:T(8,128)S(1)}, f32[32,16,1024]{2,1,0:T(8,128)}, u32[]{:S(2)}) copy-start(f32[32,16,1024]{2,1,0:T(8,128)} %get-tuple-element.68) | copy-start | bytes 6291460
  932.7 20.6 %copy-start.8 = (f32[32,16,1024]{2,1,0:T(8,128)S(1)}, f32[32,16,1024]{2,1,0:T(8,128)}, u32[]{:S(2)}) copy-start(f32[32,16,1024]{2,1,0:T(8,128)} %get-tuple-element.69) | copy-start | bytes 6291460
  953.4 20.6 %copy-start.18 = (bf16[16,16,2048]{2,1,0:T(8,128)(2,1)S(1)}, bf16[16,16,2048]{2,1,0:T(8,128)(2,1)}, u32[]{:S(2)}) copy-start(bf16[16,16,2048]{2,1,0:T(8,128)(2,1)} %get-tuple-element.42) | copy-start | bytes 3145732
  1042.1 36.6 %all-to-all-start.1 = ((bf16[32,16,2048]{2,1,0:T(8,128)(2,1)}), bf16[32,16,2048]{2,1,0:T(8,128)(2,1)S(1)}, u32[]{:S(2)}, u32[]{:S(2)}) async-start(bf16[32,16,2048]{2,1,0:T(8,128)(2,1)} %fusion.25), calls=%async_computation.1 | async-start | bytes 4194304 | tf_op jit(solution)/shard_map/all_to_all | solution.py:145
  1081.2 5.5 copy-start.14
  1081.2 5.5 copy-start.16
  1091.0 3.5 copy-start.2
  1091.0 4.1 copy-start.6
  1096.5 17.8 %copy-start.26 = (s32[512]{0:T(512)S(1)}, s32[512]{0:T(512)}, u32[]{:S(2)}) copy-start(s32[512]{0:T(512)} %copy-done.25) | copy-start | bytes 6148
  1096.5 17.8 %copy-start.28 = (pred[512]{0:T(512)(128)(4,1)S(1)}, pred[512]{0:T(512)(128)(4,1)}, u32[]{:S(2)}) copy-start(pred[512]{0:T(512)(128)(4,1)} %copy-done.27) | copy-start | bytes 1540
  1150.2 19.0 %copy-start.1 = (bf16[1,512,2048]{2,1,0:T(8,128)(2,1)S(1)}, bf16[1,512,2048]{2,1,0:T(8,128)(2,1)}, u32[]{:S(2)}) copy-start(bf16[1,512,2048]{2,1,0:T(8,128)(2,1)} %param.3) | copy-start | bytes 6291460
  (5 other events, 7.7 us)
Sparse Core Ops, SparseCore 0:
  263.2 553.7 all-gather.1
